TPU v7x, 32 devices: a whole 2x2x4 slice. The times are simulated.
32 devices in a mesh: bead: 16 (over z, y, x), space: 2 (over core).
Axes of the slice: x: 2, y: 2, z: 4, core: 2. Of those that a mesh axis runs over, the one named last changes fastest.
Arguments:
- positions: float32 [32, 3, 16384], P('bead', None, 'space'), may hold values from -6 to 6
- momenta: float32 [32, 3, 16384], P('bead', None, 'space'), may hold values from -6 to 6
- forces: float32 [32, 3, 16384], P('bead', None, 'space'), may hold values from -6 to 6
- gle_drift: float32 [32, 5, 5], replicated, may hold values from -0.25 to 0.98, as said below
- gle_noise_mix: float32 [32, 5, 5], replicated, may hold values from -1.5 to 1.5
- aux_momenta: float32 [32, 4, 3, 16384], P(None, None, None, ('space', 'bead')), may hold values from -6 to 6
- noise: float32 [2, 32, 5, 3, 16384], P(None, None, None, None, ('space', 'bead')), may hold values from -6 to 6
Outputs:
- positions_out: float32 [32, 3, 16384], P('bead', None, 'space')
- momenta_out: float32 [32, 3, 16384], P('bead', None, 'space')
- forces_out: float32 [32, 3, 16384], P('bead', None, 'space')
- aux_out: float32 [32, 4, 3, 16384], P(None, None, None, ('space', 'bead'))
Inputs may be any that keep to these rules, and one draw needn't show every extreme that they name: `gle_drift`: one matrix a mode; diagonal entries positive.
All inputs are finite; a program needn't handle non-finite values.
Results may differ from a plain program's by a relative error of at most 0.00012.
Values sent between devices are 32-bit elements; how exact they have to be, the bound alone decides.
No kernel may reach another device: no remote copies, remote signals or barrier semaphores. Data moves between devices by JAX's collectives and lax.ppermute only.
A program may use at most 64 MiB of HBM per device.

v0:
```python
import math
import jax
import jax.numpy as jnp
from jax import lax
from jax.sharding import PartitionSpec as P

BEADS = 32
CELL_ATOMS = 128
STEPS = 2
time_step = 0.5
cycle_freq = 1.5
cell_length = 2.0
pair_strength = 0.1
pair_range = 1.0


def passed_along(block, axis, distance):
    devices = range(lax.axis_size(axis))
    route = [((i - distance) % len(devices), i) for i in devices]
    return lax.ppermute(block, axis, route)


def mode_basis():
    index = jnp.arange(BEADS)
    bead_pos = index.astype(jnp.float32)[:, None]
    mode_pos = index.astype(jnp.float32)[None, :]
    phase = 2.0 * jnp.pi * bead_pos * mode_pos / BEADS
    kk = index[None, :]
    low = jnp.sqrt(1.0 / BEADS) + 0.0 * phase
    basis = jnp.where(
        kk == 0,
        low,
        jnp.where(
            kk < BEADS // 2,
            jnp.sqrt(2.0 / BEADS) * jnp.cos(phase),
            jnp.where(
                kk == BEADS // 2,
                jnp.sqrt(1.0 / BEADS) * jnp.cos(phase),
                jnp.sqrt(2.0 / BEADS) * jnp.sin(phase),
            ),
        ),
    )
    freq = 2.0 * cycle_freq * jnp.sin(jnp.pi * index.astype(jnp.float32) / BEADS)
    return (basis, freq, index)


def tile_weight(center, other):
    sa = jnp.sum(center * center, axis=1)
    sb = jnp.sum(other * other, axis=1)
    cross = jnp.einsum("xcni,xcnj->xnij", center, other, precision=lax.Precision.HIGHEST)
    dist = sa[:, :, :, None] + sb[:, :, None, :] - 2.0 * cross
    return jnp.exp(-dist / (2.0 * pair_range))


def pull(center, other):
    weight = tile_weight(center, other)
    rowsum = jnp.sum(weight, axis=3)
    pulled = jnp.einsum("xnij,xcnj->xcni", weight, other, precision=lax.Precision.HIGHEST)
    return pair_strength / pair_range * (center * rowsum[:, None] - pulled)


def mutual(center, other):
    weight = tile_weight(center, other)
    rowsum = jnp.sum(weight, axis=3)
    colsum = jnp.sum(weight, axis=2)
    pulled = jnp.einsum("xnij,xcnj->xcni", weight, other, precision=lax.Precision.HIGHEST)
    pushed = jnp.einsum("xnij,xcni->xcnj", weight, center, precision=lax.Precision.HIGHEST)
    coef = pair_strength / pair_range
    return (coef * (center * rowsum[:, None] - pulled), coef * (other * colsum[:, None] - pushed))


def moved(cells, delta):
    offset = jnp.asarray([delta * cell_length, 0.0, 0.0], dtype=cells.dtype).reshape(1, 3, 1, 1)
    return cells + offset


def pair_forces(positions):
    beads_here = positions.shape[0]
    cells = positions.shape[2] // CELL_ATOMS
    block = math.gcd(cells, 16)
    following = passed_along(positions[:, :, :CELL_ATOMS], "space", -1)
    grid = jnp.concatenate([positions, following], axis=2).reshape(
        beads_here, 3, cells + 1, CELL_ATOMS
    )

    def accumulate_pairs(number, total):
        start = number * block
        center = lax.dynamic_slice_in_dim(grid, start, block, 2)
        other = lax.dynamic_slice_in_dim(grid, start + 1, block, 2)
        own = pull(center, center)
        on_center, on_other = mutual(center, moved(other, 1))
        total = lax.dynamic_update_slice_in_dim(
            total, lax.dynamic_slice_in_dim(total, start, block, 2) + own + on_center, start, 2
        )
        return lax.dynamic_update_slice_in_dim(
            total, lax.dynamic_slice_in_dim(total, start + 1, block, 2) + on_other, start + 1, 2
        )

    total = jnp.zeros((beads_here, 3, cells + 1, CELL_ATOMS), positions.dtype)
    total = lax.fori_loop(0, cells // block, accumulate_pairs, total)
    returned = passed_along(total[:, :, cells], "space", 1)
    first = total[:, :, 0] + returned
    result = jnp.concatenate([first[:, :, None], total[:, :, 1:cells]], axis=2)
    return result.reshape(positions.shape)


def mode_step(qbeads, pbeads, aux, noise_now, basis, cosine, sinc, wsin, gle_drift, gle_noise_mix):
    qmode = jnp.einsum("jk,jcn->kcn", basis, qbeads, precision=lax.Precision.HIGHEST)
    pmode = jnp.einsum("jk,jcn->kcn", basis, pbeads, precision=lax.Precision.HIGHEST)
    state = jnp.concatenate([pmode[:, None], aux], axis=1)
    state = jnp.einsum(
        "kab,kbcn->kacn", gle_drift, state, precision=lax.Precision.HIGHEST
    ) + jnp.einsum("kab,kbcn->kacn", gle_noise_mix, noise_now, precision=lax.Precision.HIGHEST)
    pmode = state[:, 0]
    qnext = qmode * cosine + sinc * pmode
    pmode = pmode * cosine - wsin * qmode
    qbeads = jnp.einsum("jk,kcn->jcn", basis, qnext, precision=lax.Precision.HIGHEST)
    pbeads = jnp.einsum("jk,kcn->jcn", basis, pmode, precision=lax.Precision.HIGHEST)
    return (qbeads, pbeads, state[:, 1:])


def on_device(positions, momenta, forces, gle_drift, gle_noise_mix, aux_momenta, noise):
    beads_here = positions.shape[0]
    atoms_here = positions.shape[2]
    groups = lax.axis_size("bead")
    share = atoms_here // (2 * groups)
    basis, freq, index = mode_basis()
    cosine = jnp.cos(time_step * freq)[:, None, None]
    safe = jnp.where(index == 0, 1.0, freq)
    sinc = jnp.where(index == 0, time_step, jnp.sin(time_step * freq) / safe)[:, None, None]
    wsin = (freq * jnp.sin(time_step * freq))[:, None, None]
    half = 0.5 * time_step
    aux = aux_momenta
    force = forces
    for step in range(STEPS):
        momenta = momenta + half * force
        shaped_q = positions.reshape(beads_here, 3, 2, groups * share)
        shaped_p = momenta.reshape(beads_here, 3, 2, groups * share)
        owned_q, owned_p = (
            lax.all_to_all(shaped_q, "bead", split_axis=3, concat_axis=0, tiled=True),
            lax.all_to_all(shaped_p, "bead", split_axis=3, concat_axis=0, tiled=True),
        )
        new_q, new_p, aux = mode_step(
            owned_q.reshape(BEADS, 3, 2 * share),
            owned_p.reshape(BEADS, 3, 2 * share),
            aux,
            noise[step],
            basis,
            cosine,
            sinc,
            wsin,
            gle_drift,
            gle_noise_mix,
        )
        back_q, back_p = (
            lax.all_to_all(
                new_q.reshape(BEADS, 3, 2, share), "bead", split_axis=0, concat_axis=3, tiled=True
            ),
            lax.all_to_all(
                new_p.reshape(BEADS, 3, 2, share), "bead", split_axis=0, concat_axis=3, tiled=True
            ),
        )
        positions = back_q.reshape(beads_here, 3, atoms_here)
        momenta = back_p.reshape(beads_here, 3, atoms_here)
        force = pair_forces(positions)
        momenta = momenta + half * force
    return (positions, momenta, force, aux)


def solution(mesh):
    in_specs = (
        P("bead", None, "space"),
        P("bead", None, "space"),
        P("bead", None, "space"),
        P(),
        P(),
        P(None, None, None, ("space", "bead")),
        P(None, None, None, None, ("space", "bead")),
    )
    out_specs = (
        P("bead", None, "space"),
        P("bead", None, "space"),
        P("bead", None, "space"),
        P(None, None, None, ("space", "bead")),
    )
    return jax.shard_map(
        on_device, mesh=mesh, in_specs=in_specs, out_specs=out_specs, check_vma=False
    )
```

profile of v0, /device:TPU:1, one launch (start us, length us, event | category | flops | bytes accessed | tf_op | source)
XLA Modules:
  0.0 409.7 jit_solution(560465266027311314)
XLA Ops:
  2.0 8.3 %copy.360 = f32[2,3,2,4096]{1,2,0,3:T(2,128)} copy(f32[2,3,2,4096]{3,2,0,1:T(2,128)S(1)} %reshape.141) | data formatting | bytes 393216 | tf_op jit(solution)/shard_map/reshape | solution.py:138
  10.3 14.3 %reshape.167 = f32[16,1,3072]{2,1,0:T(1,128)} reshape(f32[4096,2,2,3]{3,2,1,0:T(2,128)} %bitcast.238) | data formatting | bytes 393216
  24.6 7.4 %all-to-all-start.1 = ((f32[16,1,3072]{2,1,0:T(1,128)}), f32[16,1,3072]{2,1,0:T(1,128)S(1)}, u32[]{:S(2)}, u32[]{:S(2)}) async-start(f32[16,1,3072]{2,1,0:T(1,128)} %reshape.167), calls=%async_computation.1 | async-start | bytes 393216 | tf_op jit(solution)/shard_map/all_to_all | solution.py:141
  32.7 8.3 %copy.356 = f32[2,3,2,4096]{1,2,0,3:T(2,128)} copy(f32[2,3,2,4096]{3,2,0,1:T(2,128)S(1)} %reshape.139) | data formatting | bytes 393216 | tf_op jit(solution)/shard_map/reshape | solution.py:137
  41.0 14.2 %reshape.165 = f32[16,1,3072]{2,1,0:T(1,128)} reshape(f32[4096,2,2,3]{3,2,1,0:T(2,128)} %bitcast.239) | data formatting | bytes 393216
  57.0 6.5 %all-to-all-start = ((f32[16,1,3072]{2,1,0:T(1,128)}), f32[16,1,3072]{2,1,0:T(1,128)S(1)}, u32[]{:S(2)}, u32[]{:S(2)}) async-start(f32[16,1,3072]{2,1,0:T(1,128)} %reshape.165), calls=%async_computation | async-start | bytes 393216 | tf_op jit(solution)/shard_map/all_to_all | solution.py:140
  68.3 14.8 %reshape.168 = f32[4096,2,2,3]{3,2,1,0:T(2,128)} reshape(f32[16,3072]{1,0:T(8,128)S(1)} %reduce.1) | data formatting | bytes 393216
  83.1 6.8 %copy.423 = f32[2,3,2,16,256]{4,3,2,1,0:T(8,128)S(1)} copy(f32[2,3,2,16,256]{1,2,0,4,3:T(2,128)} %bitcast.240) | data formatting | bytes 393216 | tf_op jit(solution)/shard_map/all_to_all | solution.py:141
  92.1 14.8 %reshape.166 = f32[4096,2,2,3]{3,2,1,0:T(2,128)} reshape(f32[16,3072]{1,0:T(8,128)S(1)} %reduce) | data formatting | bytes 393216
  107.0 7.0 %copy.421 = f32[2,3,2,16,256]{4,3,2,1,0:T(8,128)S(1)} copy(f32[2,3,2,16,256]{1,2,0,4,3:T(2,128)} %bitcast.241) | data formatting | bytes 393216 | tf_op jit(solution)/shard_map/all_to_all | solution.py:140
  121.2 6.4 %all-to-all-start.2 = ((f32[32,3,2,256]{3,2,1,0:T(2,128)}), f32[32,3,2,256]{3,2,1,0:T(2,128)S(1)}, u32[]{:S(2)}, u32[]{:S(2)}) async-start(f32[32,3,2,256]{3,2,1,0:T(2,128)} %copy.370), calls=%async_computation.2 | async-start | bytes 393216 | tf_op jit(solution)/shard_map/all_to_all | solution.py:156
  127.7 7.0 %all-to-all-done.2 = f32[32,3,2,256]{3,2,1,0:T(2,128)S(1)} async-done(((f32[32,3,2,256]{3,2,1,0:T(2,128)}), f32[32,3,2,256]{3,2,1,0:T(2,128)S(1)}, u32[]{:S(2)}, u32[]{:S(2)}) %all-to-all-start.2) | async-done | bytes 196640 | tf_op jit(solution)/shard_map/all_to_all | solution.py:156
  143.3 64.1 %while.32 = (s32[]{:T(128)}, f32[2,3,65,128]{3,1,2,0:T(4,128)S(1)}, f32[2,3,65,128]{3,1,2,0:T(4,128)S(1)}, s32[]{:T(128)}, s32[]{:T(128)}, /*index=5*/s32[]{:T(128)}, s32[]{:T(128)}, s32[]{:T(128)}, f32[3]{0:T(128)S(1)}) while((s32[]{:T(128)}, f32[2,3,65,128]{3,1,2,0:T(4,128)S(1)}, f32[2,3,65,128]{3,1,2,0:T(4,128)S(1)}, ...), condition=%wide.region_6.7_spmd.clone, body=%wide.region_0.6_spmd.sunk.clone.sunk | while | flops 101412872 | bytes 11750121 | solution.py:100
  207.6 8.5 %copy.428 = f32[2,3,2,16,256]{1,2,0,4,3:T(2,128)} copy(f32[2,3,2,16,256]{4,2,1,0,3:T(2,128)S(1)} %bitcast.246) | data formatting | bytes 393216 | tf_op jit(solution)/shard_map/all_to_all | solution.py:156
  216.2 14.2 %reshape.169 = f32[16,1,3072]{2,1,0:T(1,128)} reshape(f32[4096,2,2,3]{3,2,1,0:T(2,128)} %bitcast.237) | data formatting | bytes 393216
  230.4 6.6 %all-to-all-start.3 = ((f32[16,1,3072]{2,1,0:T(1,128)}), f32[16,1,3072]{2,1,0:T(1,128)S(1)}, u32[]{:S(2)}, u32[]{:S(2)}) async-start(f32[16,1,3072]{2,1,0:T(1,128)} %reshape.169), calls=%async_computation.3 | async-start | bytes 393216 | tf_op jit(solution)/shard_map/all_to_all | solution.py:140
  237.3 8.3 %copy.384 = f32[2,3,2,4096]{1,2,0,3:T(2,128)} copy(f32[2,3,2,4096]{3,2,1,0:T(2,128)S(1)} %add_add_fusion) | data formatting | bytes 393216 | tf_op jit(solution)/shard_map/add | solution.py:136
  245.6 14.2 %reshape.171 = f32[16,1,3072]{2,1,0:T(1,128)} reshape(f32[4096,2,2,3]{3,2,1,0:T(2,128)} %bitcast.242) | data formatting | bytes 393216
  269.3 14.8 %reshape.170 = f32[4096,2,2,3]{3,2,1,0:T(2,128)} reshape(f32[16,3072]{1,0:T(8,128)S(1)} %reduce.2) | data formatting | bytes 393216
  284.1 6.8 %copy.429 = f32[2,3,2,16,256]{4,3,2,1,0:T(8,128)S(1)} copy(f32[2,3,2,16,256]{1,2,0,4,3:T(2,128)} %bitcast.243) | data formatting | bytes 393216 | tf_op jit(solution)/shard_map/all_to_all | solution.py:140
  292.9 14.8 %reshape.172 = f32[4096,2,2,3]{3,2,1,0:T(2,128)} reshape(f32[16,3072]{1,0:T(8,128)S(1)} %reduce.3) | data formatting | bytes 393216
  307.7 7.3 %copy.433 = f32[2,3,2,16,256]{4,3,2,1,0:T(8,128)S(1)} copy(f32[2,3,2,16,256]{1,2,0,4,3:T(2,128)} %bitcast.244) | data formatting | bytes 393216 | tf_op jit(solution)/shard_map/all_to_all | solution.py:141
  326.8 7.0 %all-to-all-done.6 = f32[32,3,2,256]{3,2,1,0:T(2,128)S(1)} async-done(((f32[32,3,2,256]{3,2,1,0:T(2,128)}), f32[32,3,2,256]{3,2,1,0:T(2,128)S(1)}, u32[]{:S(2)}, u32[]{:S(2)}) %all-to-all-start.6) | async-done | bytes 196640 | tf_op jit(solution)/shard_map/all_to_all | solution.py:156
  342.0 63.7 %while.33 = (s32[]{:T(128)}, f32[2,3,65,128]{3,1,2,0:T(4,128)S(1)}, f32[2,3,65,128]{3,1,2,0:T(4,128)S(1)}, s32[]{:T(128)}, s32[]{:T(128)}, /*index=5*/s32[]{:T(128)}, s32[]{:T(128)}, s32[]{:T(128)}, f32[3]{0:T(128)S(1)}) while((s32[]{:T(128)}, f32[2,3,65,128]{3,1,2,0:T(4,128)S(1)}, f32[2,3,65,128]{3,1,2,0:T(4,128)S(1)}, ...), condition=%wide.region_13.14_spmd.clone, body=%wide.region_7.13_spmd.sunk.clone.sunk | while | flops 101412872 | bytes 11750121 | solution.py:100
  (171 shorter events, 188.6 us)
Async XLA Ops:
  10.3 21.9 %copy-start.8 = (f32[32,5,5]{0,2,1:T(8,128)S(1)}, f32[32,5,5]{0,2,1:T(8,128)}, u32[]{:S(2)}) copy-start(f32[32,5,5]{0,2,1:T(8,128)} %param.16) | copy-start | bytes 9604
  10.3 22.0 %copy-start.9 = (f32[32,5,5]{0,2,1:T(8,128)S(1)}, f32[32,5,5]{0,2,1:T(8,128)}, u32[]{:S(2)}) copy-start(f32[32,5,5]{0,2,1:T(8,128)} %param.17) | copy-start | bytes 9604
  10.3 22.2 %copy-start.7 = (f32[2,3,8192]{2,0,1:T(2,128)S(1)}, f32[2,3,8192]{2,0,1:T(2,128)}, u32[]{:S(2)}) copy-start(f32[2,3,8192]{2,0,1:T(2,128)} %param.13) | copy-start | bytes 589828
  24.6 32.4 %all-to-all-start.1 = ((f32[16,1,3072]{2,1,0:T(1,128)}), f32[16,1,3072]{2,1,0:T(1,128)S(1)}, u32[]{:S(2)}, u32[]{:S(2)}) async-start(f32[16,1,3072]{2,1,0:T(1,128)} %reshape.167), calls=%async_computation.1 | async-start | bytes 393216 | tf_op jit(solution)/shard_map/all_to_all | solution.py:141
  57.0 34.1 %all-to-all-start = ((f32[16,1,3072]{2,1,0:T(1,128)}), f32[16,1,3072]{2,1,0:T(1,128)S(1)}, u32[]{:S(2)}, u32[]{:S(2)}) async-start(f32[16,1,3072]{2,1,0:T(1,128)} %reshape.165), calls=%async_computation | async-start | bytes 393216 | tf_op jit(solution)/shard_map/all_to_all | solution.py:140
  114.0 3.7 copy-start
  118.9 1.0 copy-start.1
  120.3 17.7 %copy-start.2 = (f32[32,5,3,512]{3,0,2,1:T(8,128)S(1)}, f32[32,5,3,512]{3,0,2,1:T(8,128)}, u32[]{:S(2)}) copy-start(f32[32,5,3,512]{3,0,2,1:T(8,128)} %copy-done.1) | copy-start | bytes 2949124
  121.2 13.4 %all-to-all-start.2 = ((f32[32,3,2,256]{3,2,1,0:T(2,128)}), f32[32,3,2,256]{3,2,1,0:T(2,128)S(1)}, u32[]{:S(2)}, u32[]{:S(2)}) async-start(f32[32,3,2,256]{3,2,1,0:T(2,128)} %copy.370), calls=%async_computation.2 | async-start | bytes 393216 | tf_op jit(solution)/shard_map/all_to_all | solution.py:156
  127.6 15.7 %copy-start.6 = (f32[3]{0:T(128)S(1)}, f32[3]{0:T(128)}, u32[]{:S(2)}) copy-start(f32[3]{0:T(128)} %constant.208.clone..sunk.4) | copy-start | bytes 40
  134.8 8.1 %collective-permute-start = (f32[2,3,128]{2,0,1:T(2,128)S(1)}, f32[2,3,128]{2,0,1:T(2,128)S(1)}, u32[]{:S(2)}, u32[]{:S(2)}) collective-permute-start(f32[2,3,128]{2,0,1:T(2,128)S(1)} %slice.57), channel_id=1, source_target_pairs={{1,0},{0,1},{3,2},{2,3},{5,4},{4,5},{7,6},{6,7},{9,8},{8,9},{11,10... | collective-permute-start | bytes 9224 | tf_op jit(solution)/shard_map/ppermute | solution.py:20
  139.4 76.8 %all-to-all-start.4 = ((f32[32,3,2,256]{3,2,1,0:T(2,128)}), f32[32,3,2,256]{3,2,1,0:T(2,128)S(1)}, u32[]{:S(2)}, u32[]{:S(2)}) async-start(f32[32,3,2,256]{3,2,1,0:T(2,128)} %copy.376), calls=%async_computation.4 | async-start | bytes 393216 | tf_op jit(solution)/shard_map/all_to_all | solution.py:159
  207.5 29.5 %collective-permute-start.1 = (f32[2,3,128]{2,1,0:T(4,128)S(1)}, f32[2,3,128]{2,1,0:T(4,128)S(1)}, u32[]{:S(2)}, u32[]{:S(2)}) collective-permute-start(f32[2,3,128]{2,1,0:T(4,128)S(1)} %slice_bitcast_fusion.9), channel_id=1, source_target_pairs={{1,0},{0,1},{3,2},{2,3},{5,4},{4,5},{7,6},{6,7},{9,8},{8,9},{11,10... | collective-permute-start | bytes 9224 | tf_op jit(solution)/shard_map/ppermute | solution.py:20
  230.4 29.4 %all-to-all-start.3 = ((f32[16,1,3072]{2,1,0:T(1,128)}), f32[16,1,3072]{2,1,0:T(1,128)S(1)}, u32[]{:S(2)}, u32[]{:S(2)}) async-start(f32[16,1,3072]{2,1,0:T(1,128)} %reshape.169), calls=%async_computation.3 | async-start | bytes 393216 | tf_op jit(solution)/shard_map/all_to_all | solution.py:140
  259.8 31.9 %all-to-all-start.5 = ((f32[16,1,3072]{2,1,0:T(1,128)}), f32[16,1,3072]{2,1,0:T(1,128)S(1)}, u32[]{:S(2)}, u32[]{:S(2)}) async-start(f32[16,1,3072]{2,1,0:T(1,128)} %reshape.171), calls=%async_computation.5 | async-start | bytes 393216 | tf_op jit(solution)/shard_map/all_to_all | solution.py:141
  307.7 8.2 %slice-start = ((f32[32,5,3,512]{3,0,2,1:T(8,128)}), f32[32,4,3,512]{3,0,2,1:T(8,128)S(1)}, s32[]{:S(2)}) async-start(f32[32,5,3,512]{3,0,2,1:T(8,128)} %copy-done.1), calls=%async_computation.8 | async-start | bytes 1572864 | tf_op jit(solution)/shard_map/slice | solution.py:119
  319.1 18.9 %copy-start.3 = (f32[32,5,3,512]{3,0,2,1:T(8,128)}, f32[32,5,3,512]{3,0,2,1:T(8,128)S(1)}, u32[]{:S(2)}) copy-start(f32[32,5,3,512]{3,0,2,1:T(8,128)S(1)} %bitcast_add_fusion) | copy-start | bytes 2949124
  320.4 13.4 %all-to-all-start.6 = ((f32[32,3,2,256]{3,2,1,0:T(2,128)}), f32[32,3,2,256]{3,2,1,0:T(2,128)S(1)}, u32[]{:S(2)}, u32[]{:S(2)}) async-start(f32[32,3,2,256]{3,2,1,0:T(2,128)} %copy.394), calls=%async_computation.6 | async-start | bytes 393216 | tf_op jit(solution)/shard_map/all_to_all | solution.py:156
  334.0 8.0 %copy-start.4 = (f32[2,3,8192]{2,0,1:T(2,128)}, f32[2,3,8192]{2,0,1:T(2,128)S(1)}, u32[]{:S(2)}) copy-start(f32[2,3,8192]{2,0,1:T(2,128)S(1)} %reshape.151) | copy-start | bytes 589828
  334.0 7.6 %collective-permute-start.2 = (f32[2,3,128]{2,0,1:T(2,128)S(1)}, f32[2,3,128]{2,0,1:T(2,128)S(1)}, u32[]{:S(2)}, u32[]{:S(2)}) collective-permute-start(f32[2,3,128]{2,0,1:T(2,128)S(1)} %slice.62), channel_id=1, source_target_pairs={{1,0},{0,1},{3,2},{2,3},{5,4},{4,5},{7,6},{6,7},{9,8},{8,9},{11,10... | collective-permute-start | bytes 9224 | tf_op jit(solution)/shard_map/ppermute | solution.py:20
  338.0 70.2 %all-to-all-start.7 = ((f32[32,3,2,256]{3,2,1,0:T(2,128)}), f32[32,3,2,256]{3,2,1,0:T(2,128)S(1)}, u32[]{:S(2)}, u32[]{:S(2)}) async-start(f32[32,3,2,256]{3,2,1,0:T(2,128)} %copy.396), calls=%async_computation.7 | async-start | bytes 393216 | tf_op jit(solution)/shard_map/all_to_all | solution.py:159
  405.7 1.1 slice-start.1
  405.7 2.8 collective-permute-start.3
  408.7 0.8 copy-start.5
where the time goes:
time: 416 us; the launch traced here: 410 us
  local copies, waits for them, and re-layouts  190 us (46%)
  matrix products  140 us (34%)
  starting transfers between devices  52.8 us (13%)
  waiting for transfers between devices  14 us (3%)
  other arithmetic  10.1 us (2%)
    unnamed x33, local copies, waits for them, and re-layouts  119 us
    dot_general x16, matrix products, tile_weight(): jnp.einsum('xcni,xcnj->xnij', center, other, precision=lax.Precision.HIGH...  68.3 us
    dot_general x8, matrix products, mutual(): jnp.einsum('xnij,xcni->xcnj', weight, center, precision=lax.Precision.HIG...  27.2 us
    dot_general x8, matrix products, pull(): jnp.einsum('xnij,xcnj->xcni', weight, other, precision=lax.Precision.HIGH...  15.2 us
    dot_general x8, matrix products, mutual(): jnp.einsum('xnij,xcnj->xcni', weight, other, precision=lax.Precision.HIGH...  15.2 us
    all_to_all x5, local copies, waits for them, and re-layouts, on_device(): lax.all_to_all(shaped_q, 'bead', split_axis=3, concat_axis=0, tiled=True)  14.7 us
    all_to_all x4, local copies, waits for them, and re-layouts, on_device(): lax.all_to_all(shaped_p, 'bead', split_axis=3, concat_axis=0, tiled=True)  14.4 us
    all_to_all x2, waiting for transfers between devices, on_device(): lax.all_to_all(new_q.reshape(BEADS, 3, 2, share), 'bead', split_axis=0, c...  14 us
  transfers between devices with their start and end apart: 12, of which 2 were waited for; matrix products, arithmetic and copies ran while one was open for 62% of the time, Pallas kernels for 0%

commit v1 on v0

--- a/solution.py
+++ b/solution.py
@@ -138,7 +138,12 @@
         shaped_p = momenta.reshape(beads_here, 3, 2, groups * share)
         owned_q, owned_p = (
             lax.all_to_all(shaped_q, "bead", split_axis=3, concat_axis=0, tiled=True),
-            lax.all_to_all(shaped_p, "bead", split_axis=3, concat_axis=0, tiled=True),
+            jnp.concatenate(
+                lax.all_to_all(
+                    jnp.stack(jnp.split(shaped_p, lax.axis_size("bead"), axis=3)), "bead", 0, 0
+                ),
+                axis=0,
+            ),
         )
         new_q, new_p, aux = mode_step(
             owned_q.reshape(BEADS, 3, 2 * share),

time: 416 us -> 345 us (0.83)
  local copies, waits for them, and re-layouts: 190 us -> 122 us
    unnamed x33 -> x55, local copies, waits for them, and re-layouts: 119 us -> 80.6 us
    all_to_all x4 -> x2, local copies, waits for them, and re-layouts: 14.4 us -> 0.05 us  [on_device(): lax.all_to_all(jnp.stack(jnp.split(shaped_p, lax.axis_size('bead'), axis=...]
    add x1 -> x0, local copies, waits for them, and re-layouts: 8.28 us -> none  [on_device(): momenta = momenta + half * force]
    reshape x2 -> x1, local copies, waits for them, and re-layouts: 8.52 us -> 0.24 us  [on_device(): shaped_p = momenta.reshape(beads_here, 3, 2, groups * share)]
  transfers between devices with their start and end apart: 12 -> 12, of which waited for: 2 -> 3; matrix products, arithmetic and copies ran while one was open for 62% -> 65% of each run, Pallas kernels for 0% -> 0%
where the time goes in v1:
time: 345 us; the launch traced here: 340 us
  matrix products  140 us (41%)
  local copies, waits for them, and re-layouts  122 us (35%)
  starting transfers between devices  50.4 us (15%)
  waiting for transfers between devices  16.9 us (5%)
  other arithmetic  7.94 us (2%)
    unnamed x55, local copies, waits for them, and re-layouts  80.6 us
    dot_general x16, matrix products, tile_weight(): jnp.einsum('xcni,xcnj->xnij', center, other, precision=lax.Precision.HIGH...  68.3 us
    dot_general x8, matrix products, mutual(): jnp.einsum('xnij,xcni->xcnj', weight, center, precision=lax.Precision.HIG...  27.2 us
    dot_general x8, matrix products, pull(): jnp.einsum('xnij,xcnj->xcni', weight, other, precision=lax.Precision.HIGH...  15.2 us
    dot_general x8, matrix products, mutual(): jnp.einsum('xnij,xcnj->xcni', weight, other, precision=lax.Precision.HIGH...  15.2 us
    all_to_all x5, local copies, waits for them, and re-layouts, on_device(): lax.all_to_all(shaped_q, 'bead', split_axis=3, concat_axis=0, tiled=True)  14.5 us
    all_to_all x2, waiting for transfers between devices, on_device(): lax.all_to_all(new_q.reshape(BEADS, 3, 2, share), 'bead', split_axis=0, c...  14 us
    all_to_all x2, starting transfers between devices, on_device(): lax.all_to_all(jnp.stack(jnp.split(shaped_p, lax.axis_size('bead'), axis=...  13.7 us
  transfers between devices with their start and end apart: 12, of which 3 were waited for; matrix products, arithmetic and copies ran while one was open for 65% of the time, Pallas kernels for 0%

profile of v1, /device:TPU:1, one launch (start us, length us, event | category | flops | bytes accessed | tf_op | source)
XLA Modules:
  0.0 339.7 jit_solution(9942395685086071016)
XLA Ops:
  11.7 7.4 %all-to-all-start.1 = ((f32[16,2,3,2,256]{4,3,1,2,0:T(2,128)}), f32[16,2,3,2,256]{4,3,1,2,0:T(2,128)S(1)}, u32[]{:S(2)}, u32[]{:S(2)}) async-start(f32[16,2,3,2,256]{4,3,1,2,0:T(2,128)} %constant_dynamic-update-slice_fusion), calls=%async_computation.1 | async-start | bytes 393216 | tf_op jit(solution)/shard_map/all_to_all | solution.py:142
  21.2 8.3 %copy.398 = f32[2,3,2,4096]{1,2,0,3:T(2,128)} copy(f32[2,3,2,4096]{3,2,0,1:T(2,128)S(1)} %reshape.131) | data formatting | bytes 393216 | tf_op jit(solution)/shard_map/reshape | solution.py:137
  29.5 14.2 %reshape.155 = f32[16,1,3072]{2,1,0:T(1,128)} reshape(f32[4096,2,2,3]{3,2,1,0:T(2,128)} %bitcast.359) | data formatting | bytes 393216
  45.4 6.6 %all-to-all-start = ((f32[16,1,3072]{2,1,0:T(1,128)}), f32[16,1,3072]{2,1,0:T(1,128)S(1)}, u32[]{:S(2)}, u32[]{:S(2)}) async-start(f32[16,1,3072]{2,1,0:T(1,128)} %reshape.155), calls=%async_computation | async-start | bytes 393216 | tf_op jit(solution)/shard_map/all_to_all | solution.py:140
  60.6 14.8 %reshape.156 = f32[4096,2,2,3]{3,2,1,0:T(2,128)} reshape(f32[16,3072]{1,0:T(8,128)S(1)} %reduce) | data formatting | bytes 393216
  75.5 6.8 %copy.459 = f32[2,3,2,16,256]{4,3,2,1,0:T(8,128)S(1)} copy(f32[2,3,2,16,256]{1,2,0,4,3:T(2,128)} %bitcast.360) | data formatting | bytes 393216 | tf_op jit(solution)/shard_map/all_to_all | solution.py:140
  94.1 6.9 %all-to-all-done.2 = f32[32,3,2,256]{3,2,1,0:T(2,128)S(1)} async-done(((f32[32,3,2,256]{3,2,1,0:T(2,128)}), f32[32,3,2,256]{3,2,1,0:T(2,128)S(1)}, u32[]{:S(2)}, u32[]{:S(2)}) %all-to-all-start.2) | async-done | bytes 196640 | tf_op jit(solution)/shard_map/all_to_all | solution.py:161
  109.2 64.1 %while.32 = (s32[]{:T(128)}, f32[2,3,65,128]{3,1,2,0:T(4,128)S(1)}, f32[2,3,65,128]{3,1,2,0:T(4,128)S(1)}, s32[]{:T(128)}, s32[]{:T(128)}, /*index=5*/s32[]{:T(128)}, s32[]{:T(128)}, s32[]{:T(128)}, f32[3]{0:T(128)S(1)}) while((s32[]{:T(128)}, f32[2,3,65,128]{3,1,2,0:T(4,128)S(1)}, f32[2,3,65,128]{3,1,2,0:T(4,128)S(1)}, ...), condition=%wide.region_6.7_spmd.clone, body=%wide.region_0.6_spmd.sunk.clone.sunk | while | flops 101412872 | bytes 11750121 | solution.py:100
  109.8 4.5 %fusion.237 = (f32[2,16,128]{2,1,0:T(8,128)S(1)}, f32[2,16,128]{2,1,0:T(8,128)S(1)}, f32[2,16,128,128]{2,3,1,0:T(8,128)S(1)}) fusion(f32[2,3,65,128]{3,1,2,0:T(4,128)S(1)} %get-tuple-element.445, s32[]{:T(128)S(6)} %select_n.174, f32[3]{0:T(128)S(1)} %get-tuple-element.451, s32[]{:T(128)S(6)} %select_n.173, ...), kind=kOutput, calls=%fused_computation.296.clone.1 | convolution fusion | flops 22548480 | bytes 2294280 | tf_op jit(solution)/shard_map/while/body/eval_jaxpr/xcni,xcnj->xnij/dot_general | solution.py:50
  125.7 4.5 %fusion.237 = (f32[2,16,128]{2,1,0:T(8,128)S(1)}, f32[2,16,128]{2,1,0:T(8,128)S(1)}, f32[2,16,128,128]{2,3,1,0:T(8,128)S(1)}) fusion(f32[2,3,65,128]{3,1,2,0:T(4,128)S(1)} %get-tuple-element.445, s32[]{:T(128)S(6)} %select_n.174, f32[3]{0:T(128)S(1)} %get-tuple-element.451, s32[]{:T(128)S(6)} %select_n.173, ...), kind=kOutput, calls=%fused_computation.296.clone.1 | convolution fusion | flops 22548480 | bytes 2294280 | tf_op jit(solution)/shard_map/while/body/eval_jaxpr/xcni,xcnj->xnij/dot_general | solution.py:50
  141.6 4.5 %fusion.237 = (f32[2,16,128]{2,1,0:T(8,128)S(1)}, f32[2,16,128]{2,1,0:T(8,128)S(1)}, f32[2,16,128,128]{2,3,1,0:T(8,128)S(1)}) fusion(f32[2,3,65,128]{3,1,2,0:T(4,128)S(1)} %get-tuple-element.445, s32[]{:T(128)S(6)} %select_n.174, f32[3]{0:T(128)S(1)} %get-tuple-element.451, s32[]{:T(128)S(6)} %select_n.173, ...), kind=kOutput, calls=%fused_computation.296.clone.1 | convolution fusion | flops 22548480 | bytes 2294280 | tf_op jit(solution)/shard_map/while/body/eval_jaxpr/xcni,xcnj->xnij/dot_general | solution.py:50
  157.5 4.5 %fusion.237 = (f32[2,16,128]{2,1,0:T(8,128)S(1)}, f32[2,16,128]{2,1,0:T(8,128)S(1)}, f32[2,16,128,128]{2,3,1,0:T(8,128)S(1)}) fusion(f32[2,3,65,128]{3,1,2,0:T(4,128)S(1)} %get-tuple-element.445, s32[]{:T(128)S(6)} %select_n.174, f32[3]{0:T(128)S(1)} %get-tuple-element.451, s32[]{:T(128)S(6)} %select_n.173, ...), kind=kOutput, calls=%fused_computation.296.clone.1 | convolution fusion | flops 22548480 | bytes 2294280 | tf_op jit(solution)/shard_map/while/body/eval_jaxpr/xcni,xcnj->xnij/dot_general | solution.py:50
  173.5 8.5 %copy.465 = f32[2,3,2,16,256]{1,2,0,4,3:T(2,128)} copy(f32[2,3,2,16,256]{4,2,1,0,3:T(2,128)S(1)} %bitcast.363) | data formatting | bytes 393216 | tf_op jit(solution)/shard_map/all_to_all | solution.py:161
  182.2 14.2 %reshape.157 = f32[16,1,3072]{2,1,0:T(1,128)} reshape(f32[4096,2,2,3]{3,2,1,0:T(2,128)} %bitcast.358) | data formatting | bytes 393216
  196.4 6.6 %all-to-all-start.3 = ((f32[16,1,3072]{2,1,0:T(1,128)}), f32[16,1,3072]{2,1,0:T(1,128)S(1)}, u32[]{:S(2)}, u32[]{:S(2)}) async-start(f32[16,1,3072]{2,1,0:T(1,128)} %reshape.157), calls=%async_computation.3 | async-start | bytes 393216 | tf_op jit(solution)/shard_map/all_to_all | solution.py:140
  213.0 6.3 %all-to-all-start.5 = ((f32[16,2,3,2,256]{4,3,2,1,0:T(2,128)}), f32[16,2,3,2,256]{4,3,2,1,0:T(2,128)S(1)}, u32[]{:S(2)}, u32[]{:S(2)}) async-start(f32[16,2,3,2,256]{4,3,2,1,0:T(2,128)} %constant_dynamic-update-slice_fusion.16), calls=%async_computation.5 | async-start | bytes 393216 | tf_op jit(solution)/shard_map/all_to_all | solution.py:142
  222.4 14.8 %reshape.158 = f32[4096,2,2,3]{3,2,1,0:T(2,128)} reshape(f32[16,3072]{1,0:T(8,128)S(1)} %reduce.1) | data formatting | bytes 393216
  237.2 6.8 %copy.466 = f32[2,3,2,16,256]{4,3,2,1,0:T(8,128)S(1)} copy(f32[2,3,2,16,256]{1,2,0,4,3:T(2,128)} %bitcast.361) | data formatting | bytes 393216 | tf_op jit(solution)/shard_map/all_to_all | solution.py:140
  250.2 6.3 %all-to-all-start.6 = ((f32[32,3,2,256]{3,2,1,0:T(2,128)}), f32[32,3,2,256]{3,2,1,0:T(2,128)S(1)}, u32[]{:S(2)}, u32[]{:S(2)}) async-start(f32[32,3,2,256]{3,2,1,0:T(2,128)} %copy.432), calls=%async_computation.6 | async-start | bytes 393216 | tf_op jit(solution)/shard_map/all_to_all | solution.py:161
  256.6 7.0 %all-to-all-done.6 = f32[32,3,2,256]{3,2,1,0:T(2,128)S(1)} async-done(((f32[32,3,2,256]{3,2,1,0:T(2,128)}), f32[32,3,2,256]{3,2,1,0:T(2,128)S(1)}, u32[]{:S(2)}, u32[]{:S(2)}) %all-to-all-start.6) | async-done | bytes 196640 | tf_op jit(solution)/shard_map/all_to_all | solution.py:161
  271.8 63.7 %while.33 = (s32[]{:T(128)}, f32[2,3,65,128]{3,1,2,0:T(4,128)S(1)}, f32[2,3,65,128]{3,1,2,0:T(4,128)S(1)}, s32[]{:T(128)}, s32[]{:T(128)}, /*index=5*/s32[]{:T(128)}, s32[]{:T(128)}, s32[]{:T(128)}, f32[3]{0:T(128)S(1)}) while((s32[]{:T(128)}, f32[2,3,65,128]{3,1,2,0:T(4,128)S(1)}, f32[2,3,65,128]{3,1,2,0:T(4,128)S(1)}, ...), condition=%wide.region_13.14_spmd.clone, body=%wide.region_7.13_spmd.sunk.clone.sunk | while | flops 101412872 | bytes 11750121 | solution.py:100
  272.2 4.5 %fusion.247 = (f32[2,16,128]{2,1,0:T(8,128)S(1)}, f32[2,16,128]{2,1,0:T(8,128)S(1)}, f32[2,16,128,128]{2,3,1,0:T(8,128)S(1)}) fusion(f32[2,3,65,128]{3,1,2,0:T(4,128)S(1)} %get-tuple-element.472, s32[]{:T(128)S(6)} %select_n.176, f32[3]{0:T(128)S(1)} %get-tuple-element.478, s32[]{:T(128)S(6)} %select_n.175, ...), kind=kOutput, calls=%fused_computation.297.clone.1 | convolution fusion | flops 22548480 | bytes 2294280 | tf_op jit(solution)/shard_map/while/body/eval_jaxpr/xcni,xcnj->xnij/dot_general | solution.py:50
  288.1 4.5 %fusion.247 = (f32[2,16,128]{2,1,0:T(8,128)S(1)}, f32[2,16,128]{2,1,0:T(8,128)S(1)}, f32[2,16,128,128]{2,3,1,0:T(8,128)S(1)}) fusion(f32[2,3,65,128]{3,1,2,0:T(4,128)S(1)} %get-tuple-element.472, s32[]{:T(128)S(6)} %select_n.176, f32[3]{0:T(128)S(1)} %get-tuple-element.478, s32[]{:T(128)S(6)} %select_n.175, ...), kind=kOutput, calls=%fused_computation.297.clone.1 | convolution fusion | flops 22548480 | bytes 2294280 | tf_op jit(solution)/shard_map/while/body/eval_jaxpr/xcni,xcnj->xnij/dot_general | solution.py:50
  303.9 4.5 %fusion.247 = (f32[2,16,128]{2,1,0:T(8,128)S(1)}, f32[2,16,128]{2,1,0:T(8,128)S(1)}, f32[2,16,128,128]{2,3,1,0:T(8,128)S(1)}) fusion(f32[2,3,65,128]{3,1,2,0:T(4,128)S(1)} %get-tuple-element.472, s32[]{:T(128)S(6)} %select_n.176, f32[3]{0:T(128)S(1)} %get-tuple-element.478, s32[]{:T(128)S(6)} %select_n.175, ...), kind=kOutput, calls=%fused_computation.297.clone.1 | convolution fusion | flops 22548480 | bytes 2294280 | tf_op jit(solution)/shard_map/while/body/eval_jaxpr/xcni,xcnj->xnij/dot_general | solution.py:50
  (191 shorter events, 169.4 us)
Async XLA Ops:
  0.6 20.4 %copy-start.7 = (f32[2,3,8192]{2,0,1:T(2,128)S(1)}, f32[2,3,8192]{2,0,1:T(2,128)}, u32[]{:S(2)}) copy-start(f32[2,3,8192]{2,0,1:T(2,128)} %param.13) | copy-start | bytes 589828
  11.7 33.7 %all-to-all-start.1 = ((f32[16,2,3,2,256]{4,3,1,2,0:T(2,128)}), f32[16,2,3,2,256]{4,3,1,2,0:T(2,128)S(1)}, u32[]{:S(2)}, u32[]{:S(2)}) async-start(f32[16,2,3,2,256]{4,3,1,2,0:T(2,128)} %constant_dynamic-update-slice_fusion), calls=%async_computation.1 | async-start | bytes 393216 | tf_op jit(solution)/shard_map/all_to_all | solution.py:142
  45.4 13.6 %all-to-all-start = ((f32[16,1,3072]{2,1,0:T(1,128)}), f32[16,1,3072]{2,1,0:T(1,128)S(1)}, u32[]{:S(2)}, u32[]{:S(2)}) async-start(f32[16,1,3072]{2,1,0:T(1,128)} %reshape.155), calls=%async_computation | async-start | bytes 393216 | tf_op jit(solution)/shard_map/all_to_all | solution.py:140
  82.3 3.7 %copy-start = (f32[32,5,3,512]{3,1,2,0:T(8,128)S(1)}, f32[32,5,3,512]{3,1,2,0:T(8,128)}, u32[]{:S(2)}) copy-start(f32[32,5,3,512]{3,1,2,0:T(8,128)} %fusion.43) | copy-start | bytes 2949124
  87.2 1.0 copy-start.1
  88.6 15.3 %copy-start.2 = (f32[32,5,3,512]{3,0,2,1:T(8,128)S(1)}, f32[32,5,3,512]{3,0,2,1:T(8,128)}, u32[]{:S(2)}) copy-start(f32[32,5,3,512]{3,0,2,1:T(8,128)} %copy-done.1) | copy-start | bytes 2949124
  89.5 11.5 %all-to-all-start.2 = ((f32[32,3,2,256]{3,2,1,0:T(2,128)}), f32[32,3,2,256]{3,2,1,0:T(2,128)S(1)}, u32[]{:S(2)}, u32[]{:S(2)}) async-start(f32[32,3,2,256]{3,2,1,0:T(2,128)} %copy.410), calls=%async_computation.2 | async-start | bytes 393216 | tf_op jit(solution)/shard_map/all_to_all | solution.py:161
  94.0 15.2 %copy-start.6 = (f32[3]{0:T(128)S(1)}, f32[3]{0:T(128)}, u32[]{:S(2)}) copy-start(f32[3]{0:T(128)} %constant.208.clone..sunk.4) | copy-start | bytes 40
  101.2 7.6 %collective-permute-start = (f32[2,3,128]{2,0,1:T(2,128)S(1)}, f32[2,3,128]{2,0,1:T(2,128)S(1)}, u32[]{:S(2)}, u32[]{:S(2)}) collective-permute-start(f32[2,3,128]{2,0,1:T(2,128)S(1)} %slice.57), channel_id=1, source_target_pairs={{1,0},{0,1},{3,2},{2,3},{5,4},{4,5},{7,6},{6,7},{9,8},{8,9},{11,10... | collective-permute-start | bytes 9224 | tf_op jit(solution)/shard_map/ppermute | solution.py:20
  105.2 76.7 %all-to-all-start.4 = ((f32[32,3,2,256]{3,2,1,0:T(2,128)}), f32[32,3,2,256]{3,2,1,0:T(2,128)S(1)}, u32[]{:S(2)}, u32[]{:S(2)}) async-start(f32[32,3,2,256]{3,2,1,0:T(2,128)} %copy.416), calls=%async_computation.4 | async-start | bytes 393216 | tf_op jit(solution)/shard_map/all_to_all | solution.py:164
  173.4 29.6 %collective-permute-start.1 = (f32[2,3,128]{2,1,0:T(4,128)S(1)}, f32[2,3,128]{2,1,0:T(4,128)S(1)}, u32[]{:S(2)}, u32[]{:S(2)}) collective-permute-start(f32[2,3,128]{2,1,0:T(4,128)S(1)} %slice_bitcast_fusion.41), channel_id=1, source_target_pairs={{1,0},{0,1},{3,2},{2,3},{5,4},{4,5},{7,6},{6,7},{9,8},{8,9},{11,10... | collective-permute-start | bytes 9224 | tf_op jit(solution)/shard_map/ppermute | solution.py:20
  196.4 16.6 %all-to-all-start.3 = ((f32[16,1,3072]{2,1,0:T(1,128)}), f32[16,1,3072]{2,1,0:T(1,128)S(1)}, u32[]{:S(2)}, u32[]{:S(2)}) async-start(f32[16,1,3072]{2,1,0:T(1,128)} %reshape.157), calls=%async_computation.3 | async-start | bytes 393216 | tf_op jit(solution)/shard_map/all_to_all | solution.py:140
  213.0 32.0 %all-to-all-start.5 = ((f32[16,2,3,2,256]{4,3,2,1,0:T(2,128)}), f32[16,2,3,2,256]{4,3,2,1,0:T(2,128)S(1)}, u32[]{:S(2)}, u32[]{:S(2)}) async-start(f32[16,2,3,2,256]{4,3,2,1,0:T(2,128)} %constant_dynamic-update-slice_fusion.16), calls=%async_computation.5 | async-start | bytes 393216 | tf_op jit(solution)/shard_map/all_to_all | solution.py:142
  244.1 1.6 slice-start
  248.9 18.9 %copy-start.3 = (f32[32,5,3,512]{3,0,2,1:T(8,128)}, f32[32,5,3,512]{3,0,2,1:T(8,128)S(1)}, u32[]{:S(2)}) copy-start(f32[32,5,3,512]{3,0,2,1:T(8,128)S(1)} %bitcast_add_fusion) | copy-start | bytes 2949124
  250.2 13.4 %all-to-all-start.6 = ((f32[32,3,2,256]{3,2,1,0:T(2,128)}), f32[32,3,2,256]{3,2,1,0:T(2,128)S(1)}, u32[]{:S(2)}, u32[]{:S(2)}) async-start(f32[32,3,2,256]{3,2,1,0:T(2,128)} %copy.432), calls=%async_computation.6 | async-start | bytes 393216 | tf_op jit(solution)/shard_map/all_to_all | solution.py:161
  263.8 8.0 %copy-start.4 = (f32[2,3,8192]{2,0,1:T(2,128)}, f32[2,3,8192]{2,0,1:T(2,128)S(1)}, u32[]{:S(2)}) copy-start(f32[2,3,8192]{2,0,1:T(2,128)S(1)} %reshape.141) | copy-start | bytes 589828
  263.8 7.5 %collective-permute-start.2 = (f32[2,3,128]{2,0,1:T(2,128)S(1)}, f32[2,3,128]{2,0,1:T(2,128)S(1)}, u32[]{:S(2)}, u32[]{:S(2)}) collective-permute-start(f32[2,3,128]{2,0,1:T(2,128)S(1)} %slice.62), channel_id=1, source_target_pairs={{1,0},{0,1},{3,2},{2,3},{5,4},{4,5},{7,6},{6,7},{9,8},{8,9},{11,10... | collective-permute-start | bytes 9224 | tf_op jit(solution)/shard_map/ppermute | solution.py:20
  267.9 70.2 %all-to-all-start.7 = ((f32[32,3,2,256]{3,2,1,0:T(2,128)}), f32[32,3,2,256]{3,2,1,0:T(2,128)S(1)}, u32[]{:S(2)}, u32[]{:S(2)}) async-start(f32[32,3,2,256]{3,2,1,0:T(2,128)} %copy.434), calls=%async_computation.7 | async-start | bytes 393216 | tf_op jit(solution)/shard_map/all_to_all | solution.py:164
  335.5 1.1 slice-start.1
  335.6 2.8 collective-permute-start.3
  338.5 0.8 copy-start.5
